TPU v7x, 32 devices: a whole 2x2x4 slice. The times are simulated.
32 devices in a mesh: grp: 16 (over z, y, x), row: 2 (over core).
Axes of the slice: x: 2, y: 2, z: 4, core: 2. Of those that a mesh axis runs over, the one named last changes fastest.
Arguments:
- image_rows: bfloat16 [64, 16, 16, 512], P('grp', 'row'), may hold values from -6 to 6
- grad_out: bfloat16 [64, 16, 16, 512], P(('grp', 'row')), may hold values from -6 to 6
- code_ids: int32 [16384], P(('grp', 'row')), may hold values from 0 to 1023
- dead_flags: int32 [1024], replicated, may hold values from 0 to 1, as said below
- replace_ids: int32 [1024], replicated, may hold values from 0 to 16383
- latents: bfloat16 [16384, 256], P(('grp', 'row')), may hold values from -6 to 6
- codebook: float32 [1024, 256], P(('grp', 'row')), may hold values from -6 to 6
- norm1_gain: bfloat16 [512], replicated, may hold values from 0.5 to 1.5
- norm1_bias: bfloat16 [512], replicated, may hold values from -3 to 3
- conv1_kernel: bfloat16 [3, 3, 512, 512], replicated, may hold values from -0.09375 to 0.09375
- conv1_bias: bfloat16 [512], replicated, may hold values from -3 to 3
- norm2_gain: bfloat16 [512], replicated, may hold values from 0.5 to 1.5
- norm2_bias: bfloat16 [512], replicated, may hold values from -3 to 3
- conv2_kernel: bfloat16 [3, 3, 512, 512], replicated, may hold values from -0.09375 to 0.09375
- conv2_bias: bfloat16 [512], replicated, may hold values from -3 to 3
- norm3_gain: bfloat16 [512], replicated, may hold values from 0.5 to 1.5
- norm3_bias: bfloat16 [512], replicated, may hold values from -3 to 3
- query_weight: bfloat16 [512, 512], replicated, may hold values from -0.25 to 0.25
- query_bias: bfloat16 [512], replicated, may hold values from -3 to 3
- key_weight: bfloat16 [512, 512], replicated, may hold values from -0.25 to 0.25
- value_weight: bfloat16 [512, 512], replicated, may hold values from -0.25 to 0.25
- value_bias: bfloat16 [512], replicated, may hold values from -3 to 3
- out_weight: bfloat16 [512, 512], replicated, may hold values from -2 to 2
- out_bias: bfloat16 [512], replicated, may hold values from -3 to 3
Outputs:
- block_out: bfloat16 [64, 16, 16, 512], P(('grp', 'row'))
- input_grad: bfloat16 [64, 16, 16, 512], P('grp', 'row')
- norm1_gain_grad: float32 [512], replicated
- norm1_bias_grad: float32 [512], replicated
- conv1_kernel_grad: float32 [3, 3, 512, 512], replicated
- conv1_bias_grad: float32 [512], replicated
- norm2_gain_grad: float32 [512], replicated
- norm2_bias_grad: float32 [512], replicated
- conv2_kernel_grad: float32 [3, 3, 512, 512], replicated
- conv2_bias_grad: float32 [512], replicated
- norm3_gain_grad: float32 [512], replicated
- norm3_bias_grad: float32 [512], replicated
- query_weight_grad: float32 [512, 512], replicated
- query_bias_grad: float32 [512], replicated
- key_weight_grad: float32 [512, 512], replicated
- value_weight_grad: float32 [512, 512], replicated
- value_bias_grad: float32 [512], replicated
- out_weight_grad: float32 [512, 512], replicated
- out_bias_grad: float32 [512], replicated
- new_codebook: float32 [1024, 256], P(('grp', 'row'))
- usage: int32 [1024], replicated
- perplexity: float32 [], replicated
Inputs may be any that keep to these rules, and one draw needn't show every extreme that they name: `code_ids`: a code index. `dead_flags`: exactly 256 entries are 1, the others 0. `replace_ids`: a row of latents.
All inputs are finite; a program needn't handle non-finite values.
Results may differ from a plain program's by a relative error of at most 0.014.
The roundings to bfloat16 on the way count: a program that leaves them out, or rounds other values in their place, can miss the bound.
Values may be sent and summed in bfloat16 or wider, within the bound.
No kernel may reach another device: no remote copies, remote signals or barrier semaphores. Data moves between devices by JAX's collectives and lax.ppermute only.
A program may use at most 128 MiB of HBM per device.

v0:
```python
import jax
import jax.numpy as jnp
from jax import lax
from jax.sharding import PartitionSpec as P

G = 32
epsilon = 1e-06


def group_norm(source, scaling, offsets):
    images, height, across, channels = source.shape
    grouped = source.reshape(images, height * across, G, channels // G)
    middle = jnp.mean(grouped, axis=(1, 3), keepdims=True)
    centered = grouped - middle
    spread = jnp.mean(centered * centered, axis=(1, 3), keepdims=True)
    normed = (centered * lax.rsqrt(spread + epsilon)).reshape(images, height, across, channels)
    return normed * scaling + offsets


def norm_swish(source, scaling, offsets):
    return jax.nn.silu(group_norm(source, scaling, offsets))


def padded(source):
    return jnp.pad(source, ((0, 0), (1, 1), (1, 1), (0, 0)))


def conv_taps(source, kernel):
    images, height, across, channels = source.shape
    border = padded(source)
    summed = jnp.zeros((images, height, across, kernel.shape[3]), jnp.float32)
    for tap_row in range(3):
        for tap_col in range(3):
            window = border[:, tap_row : tap_row + height, tap_col : tap_col + across, :]
            summed = summed + lax.dot_general(
                window,
                kernel[tap_row, tap_col],
                (((3,), (0,)), ((), ())),
                preferred_element_type=jnp.float32,
            )
    return summed


def kernel_grad(source, upstream):
    images, height, across, channels = source.shape
    border = padded(source)
    pieces = []
    for tap_row in range(3):
        for tap_col in range(3):
            window = border[:, tap_row : tap_row + height, tap_col : tap_col + across, :]
            pieces.append(
                lax.dot_general(
                    window,
                    upstream,
                    (((0, 1, 2), (0, 1, 2)), ((), ())),
                    preferred_element_type=jnp.float32,
                )
            )
    return jnp.stack(pieces).reshape(3, 3, channels, upstream.shape[3])


def flip_kernel(kernel):
    return jnp.transpose(kernel[::-1, ::-1], (0, 1, 3, 2))


def local(
    image_rows,
    grad_out,
    code_ids,
    dead_flags,
    replace_ids,
    latents,
    codebook,
    norm1_gain,
    norm1_bias,
    conv1_kernel,
    conv1_bias,
    norm2_gain,
    norm2_bias,
    conv2_kernel,
    conv2_bias,
    norm3_gain,
    norm3_bias,
    query_weight,
    query_bias,
    key_weight,
    value_weight,
    value_bias,
    out_weight,
    out_bias,
):
    (
        first_gain,
        first_offset,
        first_bias,
        second_gain,
        second_offset,
        second_bias,
        third_gain,
        third_offset,
        query_offset,
        value_offset,
        out_offset,
    ) = [
        vector.astype(jnp.float32)
        for vector in (
            norm1_gain,
            norm1_bias,
            conv1_bias,
            norm2_gain,
            norm2_bias,
            conv2_bias,
            norm3_gain,
            norm3_bias,
            query_bias,
            value_bias,
            out_bias,
        )
    ]
    regrouped = lax.all_to_all(image_rows, "row", split_axis=0, concat_axis=1, tiled=True)
    images, height, across, channels = regrouped.shape
    positions = height * across
    pixels = images * positions
    key_scale = channels ** (-0.5)
    contract_rows = (((0,), (0,)), ((), ()))
    contract_cols = (((1,), (1,)), ((), ()))
    source = regrouped.astype(jnp.float32)
    first_active = norm_swish(source, first_gain, first_offset).astype(jnp.bfloat16)
    first_filtered = conv_taps(first_active, conv1_kernel) + first_bias
    second_active = norm_swish(first_filtered, second_gain, second_offset).astype(jnp.bfloat16)
    residual = source + (conv_taps(second_active, conv2_kernel) + second_bias)
    normed = (
        group_norm(residual, third_gain, third_offset)
        .astype(jnp.bfloat16)
        .reshape(pixels, channels)
    )
    queries = (
        (jnp.dot(normed, query_weight, preferred_element_type=jnp.float32) + query_offset)
        .astype(jnp.bfloat16)
        .reshape(images, positions, channels)
    )
    key_rows = (
        jnp.dot(normed, key_weight, preferred_element_type=jnp.float32)
        .astype(jnp.bfloat16)
        .reshape(images, positions, channels)
    )
    values = (
        (jnp.dot(normed, value_weight, preferred_element_type=jnp.float32) + value_offset)
        .astype(jnp.bfloat16)
        .reshape(images, positions, channels)
    )
    scores = (
        jnp.einsum("bnd,bmd->bnm", queries, key_rows, preferred_element_type=jnp.float32)
        * key_scale
    )
    peak_score = jnp.max(scores, axis=2, keepdims=True)
    lifted = jnp.exp(scores - peak_score)
    summed = jnp.sum(lifted, axis=2, keepdims=True)
    log_total = peak_score + jnp.log(summed)
    attention_low = (lifted / summed).astype(jnp.bfloat16)
    blended = (
        jnp.einsum("bnm,bmd->bnd", attention_low, values, preferred_element_type=jnp.float32)
        .astype(jnp.bfloat16)
        .reshape(pixels, channels)
    )
    projected = jnp.dot(blended, out_weight, preferred_element_type=jnp.float32) + out_offset
    block_out = (residual + projected.reshape(images, height, across, channels)).astype(
        jnp.bfloat16
    )
    upstream = grad_out.reshape(pixels, channels)
    out_bias_grad = jnp.sum(upstream.astype(jnp.float32), axis=0)
    out_weight_grad = lax.dot_general(
        blended, upstream, contract_rows, preferred_element_type=jnp.float32
    )
    grad_blended = (
        lax.dot_general(upstream, out_weight, contract_cols, preferred_element_type=jnp.float32)
        .astype(jnp.bfloat16)
        .reshape(images, positions, channels)
    )
    rescored = (
        jnp.einsum("bnd,bmd->bnm", queries, key_rows, preferred_element_type=jnp.float32)
        * key_scale
    )
    attention = jnp.exp(rescored - log_total)
    grad_values = (
        jnp.einsum(
            "bnm,bnd->bmd",
            attention.astype(jnp.bfloat16),
            grad_blended,
            preferred_element_type=jnp.float32,
        )
        .astype(jnp.bfloat16)
        .reshape(pixels, channels)
    )
    grad_attention = jnp.einsum(
        "bnd,bmd->bnm", grad_blended, values, preferred_element_type=jnp.float32
    )
    grad_scores = (
        attention * (grad_attention - jnp.sum(attention * grad_attention, axis=2, keepdims=True))
    ).astype(jnp.bfloat16)
    grad_queries = (
        (
            jnp.einsum("bnm,bmd->bnd", grad_scores, key_rows, preferred_element_type=jnp.float32)
            * key_scale
        )
        .astype(jnp.bfloat16)
        .reshape(pixels, channels)
    )
    grad_keys = (
        (
            jnp.einsum("bnm,bnd->bmd", grad_scores, queries, preferred_element_type=jnp.float32)
            * key_scale
        )
        .astype(jnp.bfloat16)
        .reshape(pixels, channels)
    )
    query_bias_grad = jnp.sum(grad_queries.astype(jnp.float32), axis=0)
    value_bias_grad = jnp.sum(grad_values.astype(jnp.float32), axis=0)
    query_weight_grad = lax.dot_general(
        normed, grad_queries, contract_rows, preferred_element_type=jnp.float32
    )
    key_weight_grad = lax.dot_general(
        normed, grad_keys, contract_rows, preferred_element_type=jnp.float32
    )
    value_weight_grad = lax.dot_general(
        normed, grad_values, contract_rows, preferred_element_type=jnp.float32
    )
    grad_normed = lax.dot_general(
        grad_queries, query_weight, contract_cols, preferred_element_type=jnp.float32
    )
    grad_normed = grad_normed + lax.dot_general(
        grad_keys, key_weight, contract_cols, preferred_element_type=jnp.float32
    )
    grad_normed = grad_normed + lax.dot_general(
        grad_values, value_weight, contract_cols, preferred_element_type=jnp.float32
    )
    skipped, third_pull = jax.vjp(group_norm, residual, third_gain, third_offset)
    grad_residual, third_gain_grad, third_offset_grad = third_pull(
        grad_normed.reshape(images, height, across, channels)
    )
    grad_residual = grad_residual + grad_out.astype(jnp.float32)
    grad_second_out = grad_residual.astype(jnp.bfloat16)
    second_bias_grad = jnp.sum(grad_second_out.astype(jnp.float32), axis=(0, 1, 2))
    conv2_kernel_grad = kernel_grad(second_active, grad_second_out)
    grad_second = conv_taps(grad_second_out, flip_kernel(conv2_kernel))
    skipped, second_pull = jax.vjp(norm_swish, first_filtered, second_gain, second_offset)
    grad_first_filtered, second_gain_grad, second_offset_grad = second_pull(grad_second)
    grad_first_out = grad_first_filtered.astype(jnp.bfloat16)
    first_bias_grad = jnp.sum(grad_first_out.astype(jnp.float32), axis=(0, 1, 2))
    conv1_kernel_grad = kernel_grad(first_active, grad_first_out)
    grad_first = conv_taps(grad_first_out, flip_kernel(conv1_kernel))
    skipped, first_pull = jax.vjp(norm_swish, source, first_gain, first_offset)
    grad_source, first_gain_grad, first_offset_grad = first_pull(grad_first)
    input_local = (grad_residual + grad_source).astype(jnp.bfloat16)
    input_grad = lax.all_to_all(input_local, "row", split_axis=1, concat_axis=0, tiled=True)
    code_range = jnp.arange(dead_flags.shape[0], dtype=jnp.int32)
    counts = jnp.sum((code_ids[:, None] == code_range[None, :]).astype(jnp.float32), axis=0)
    (
        first_gain_grad,
        first_offset_grad,
        conv1_kernel_grad,
        first_bias_grad,
        second_gain_grad,
        second_offset_grad,
        conv2_kernel_grad,
        second_bias_grad,
        counts,
        third_gain_grad,
        third_offset_grad,
        query_weight_grad,
        query_bias_grad,
        key_weight_grad,
        value_weight_grad,
        value_bias_grad,
        out_weight_grad,
        out_bias_grad,
    ) = lax.psum(
        (
            first_gain_grad,
            first_offset_grad,
            conv1_kernel_grad,
            first_bias_grad,
            second_gain_grad,
            second_offset_grad,
            conv2_kernel_grad,
            second_bias_grad,
            counts,
            third_gain_grad,
            third_offset_grad,
            query_weight_grad,
            query_bias_grad,
            key_weight_grad,
            value_weight_grad,
            value_bias_grad,
            out_weight_grad,
            out_bias_grad,
        ),
        ("grp", "row"),
    )
    shares = counts / jnp.sum(counts)
    perplexity = jnp.exp(-jnp.sum(shares * jnp.log(shares + 1e-10)))
    usage = counts.astype(jnp.int32)
    local_pixels = latents.shape[0]
    book_rows = codebook.shape[0]
    device_index = lax.axis_index(("grp", "row"))
    pixel_offset = device_index * local_pixels
    pixel_range = jnp.arange(local_pixels, dtype=jnp.int32)
    own_flags = lax.dynamic_slice_in_dim(dead_flags, device_index * book_rows, book_rows)
    wanted = replace_ids - pixel_offset
    chosen = (wanted[:, None] == pixel_range[None, :]).astype(jnp.bfloat16)
    fetched = lax.psum_scatter(
        jnp.dot(chosen, latents, preferred_element_type=jnp.float32),
        ("grp", "row"),
        scatter_dimension=0,
        tiled=True,
    )
    new_codebook = jnp.where(own_flags[:, None] == 1, fetched, codebook)
    return (
        block_out,
        input_grad,
        first_gain_grad,
        first_offset_grad,
        conv1_kernel_grad,
        first_bias_grad,
        second_gain_grad,
        second_offset_grad,
        conv2_kernel_grad,
        second_bias_grad,
        third_gain_grad,
        third_offset_grad,
        query_weight_grad,
        query_bias_grad,
        key_weight_grad,
        value_weight_grad,
        value_bias_grad,
        out_weight_grad,
        out_bias_grad,
        new_codebook,
        usage,
        perplexity,
    )


def solution(mesh):
    in_specs = (
        P("grp", "row", None, None),
        P(("grp", "row"), None, None, None),
        P(("grp", "row")),
        P(),
        P(),
        P(("grp", "row"), None),
        P(("grp", "row"), None),
        P(),
        P(),
        P(),
        P(),
        P(),
        P(),
        P(),
        P(),
        P(),
        P(),
        P(),
        P(),
        P(),
        P(),
        P(),
        P(),
        P(),
    )
    out_specs = (
        P(("grp", "row"), None, None, None),
        P("grp", "row", None, None),
        P(),
        P(),
        P(),
        P(),
        P(),
        P(),
        P(),
        P(),
        P(),
        P(),
        P(),
        P(),
        P(),
        P(),
        P(),
        P(),
        P(),
        P(("grp", "row"), None),
        P(),
        P(),
    )
    return jax.shard_map(local, mesh=mesh, in_specs=in_specs, out_specs=out_specs, check_vma=False)
```

profile of v0, /device:TPU:0, one launch (start us, length us, event | category | flops | bytes accessed | tf_op | source)
XLA Modules:
  0.0 556.4 jit_solution(8809578873958543179)
XLA Ops:
  7.2 3.6 all-to-all-start
  11.6 2.4 fusion
  32.0 1.7 fusion.43
  40.6 5.3 reshape.298
  49.5 1.7 convolution_convert_fusion.1
  55.7 6.6 %copy.106 = bf16[3,3,512,512]{2,3,1,0:T(8,128)(2,1)} copy(bf16[3,3,512,512]{3,2,1,0:T(8,128)(2,1)} %param.37) | data formatting | bytes 9437184 | tf_op args[13]
  62.3 2.3 convolution_convert_fusion.2
  64.6 2.6 fusion.139
  68.8 6.1 %copy.103 = f32[2,256,32,16]{1,0,3,2:T(2,128)} copy(f32[2,256,32,16]{3,2,1,0:T(8,128)} %reshape.298) | data formatting | bytes 2097152 | tf_op jit(solution)/shard_map/reshape | solution.py:12
  74.9 2.6 fusion.141
  77.5 2.0 convolution_add_fusion.17
  82.6 2.5 copy.100
  85.1 2.9 reshape.297
  88.2 2.9 fusion.27
  91.6 2.8 reverse_bitcast_fusion.1
  99.8 1.9 fusion.133
  102.1 1.9 multiply_reduce_fusion.1
  104.4 1.9 convert_reduce_fusion.5
  113.9 3.3 copy-done.13
  122.7 3.7 copy-done.12
  126.4 6.9 %copy.107 = bf16[3,3,512,512]{2,3,1,0:T(8,128)(2,1)} copy(bf16[3,3,512,512]{3,2,1,0:T(8,128)(2,1)} %param.33) | data formatting | bytes 9437184 | tf_op args[9]
  133.3 2.7 reverse_bitcast_fusion
  139.6 1.9 fusion.134
  141.9 1.6 multiply_reduce_fusion.2
  143.9 1.6 convolution_add_fusion.18
  145.5 3.1 add_convert_fusion
  149.5 3.5 all-to-all-start.1
  155.8 44.5 %all-reduce.4 = (f32[512]{0:T(512)}, f32[512]{0:T(512)}, f32[512]{0:T(512)}, f32[512]{0:T(512)}, f32[512]{0:T(512)}, /*index=5*/f32[512]{0:T(512)}, f32[512]{0:T...) all-reduce(f32[512]{0:T(512)S(1)} %get-tuple-element.24, ...), channel_id=1, replica_groups=mesh['grp'=16,'row'=2] {'grp','row'}, use_global_device_ids=true, to_apply=%region_27.28 | all-reduce | flops 6656 | bytes 53248 | tf_op jit(solution)/shard_map/psum | solution.py:277
  200.9 1.8 multiply_reduce_fusion.10
  205.7 325.8 %all-reduce.8.cloned.1.call-done = (f32[3,3,512,512]{3,2,1,0:T(8,128)}, f32[3,3,512,512]{3,2,1,0:T(8,128)}, f32[512,512]{1,0:T(8,128)}, f32[512,512]{1,0:T(8,128...) async-done(((f32[3,3,512,512]{3,2,1,0:T(8,128)}, f32[3,3,512,512]{3,2,1,0:T(8,128)}, f32[512,512]{1,0:T(8,128)}, f32[512,512]{1,0:T(8,128)}, f32[512,512]{1,0:T(8,128)}, ...) | async-done | bytes 23068688 | tf_op jit(solution)/shard_map/psum | solution.py:277
  531.5 8.8 %copy.191 = f32[3,3,512,512]{3,2,1,0:T(8,128)} copy(f32[3,3,512,512]{3,2,1,0:T(8,128)} %get-tuple-element.78) | data formatting | bytes 18874368
  540.3 4.1 copy.192
  (260 shorter events, 72.3 us)
Async XLA Ops:
  7.2 44.0 %copy-start = (bf16[512,512]{1,0:T(8,128)(2,1)S(1)}, bf16[512,512]{1,0:T(8,128)(2,1)}, u32[]{:S(2)}) copy-start(bf16[512,512]{1,0:T(8,128)(2,1)} %param.44) | copy-start | bytes 1572868
  7.2 8.3 %copy-start.31 = (bf16[512]{0:T(512)(128)(2,1)S(1)}, bf16[512]{0:T(512)(128)(2,1)}, u32[]{:S(2)}) copy-start(bf16[512]{0:T(512)(128)(2,1)} %param.32) | copy-start | bytes 3076
  7.2 9.3 %copy-start.32 = (bf16[512]{0:T(512)(128)(2,1)S(1)}, bf16[512]{0:T(512)(128)(2,1)}, u32[]{:S(2)}) copy-start(bf16[512]{0:T(512)(128)(2,1)} %param.35) | copy-start | bytes 3076
  7.2 9.3 %copy-start.33 = (bf16[512]{0:T(512)(128)(2,1)S(1)}, bf16[512]{0:T(512)(128)(2,1)}, u32[]{:S(2)}) copy-start(bf16[512]{0:T(512)(128)(2,1)} %param.34) | copy-start | bytes 3076
  7.2 7.6 %all-to-all-start = ((bf16[4,8,16,512]{3,2,1,0:T(8,128)(2,1)}), bf16[4,8,16,512]{3,2,1,0:T(8,128)(2,1)S(1)}, u32[]{:S(2)}, u32[]{:S(2)}) async-start(bf16[4,8,16,512]{3,2,1,0:T(8,128)(2,1)} %param.24), calls=%async_computation | async-start | bytes 1048576 | tf_op jit(solution)/shard_map/all_to_all | solution.py:120
  10.9 193.4 %reduce-scatter.2.cloned.1.call-start = ((), (), s32[]{:S(2)}) async-start(), calls=%async_computation.3 | async-start | bytes 1081344 | tf_op jit(solution)/shard_map/reduce_scatter | solution.py:311
  14.1 517.4 %all-reduce.8.cloned.1.call-start = ((), (), s32[]{:S(2)}) async-start(), calls=%async_computation.4 | async-start | bytes 46137344 | tf_op jit(solution)/shard_map/psum | solution.py:277
  14.9 4.9 copy-start.2
  26.2 4.9 copy-start.34
  26.3 5.4 copy-start.35
  30.8 6.0 %copy-start.5 = (f32[2,16,16,512]{3,2,1,0:T(8,128)}, f32[2,16,16,512]{3,2,1,0:T(8,128)S(1)}, u32[]{:S(2)}) copy-start(f32[2,16,16,512]{3,2,1,0:T(8,128)S(1)} %get-tuple-element.60) | copy-start | bytes 3145732
  31.7 6.6 %slice-start = ((s8[4718592]{0:T(1024)(128)(4,1)}), s8[4194304]{0:T(1024)(128)(4,1)S(1)}, s32[]{:S(2)}) async-start(s8[4718592]{0:T(1024)(128)(4,1)} %bitcast.513), calls=%async_computation.5 | async-start | bytes 8388608
  33.7 4.6 slice-start.1
  40.6 6.2 %copy-start.29 = (bf16[512]{0:T(512)(128)(2,1)S(1)}, bf16[512]{0:T(512)(128)(2,1)}, u32[]{:S(2)}) copy-start(bf16[512]{0:T(512)(128)(2,1)} %param.39) | copy-start | bytes 3076
  40.6 6.2 %copy-start.36 = (bf16[512]{0:T(512)(128)(2,1)S(1)}, bf16[512]{0:T(512)(128)(2,1)}, u32[]{:S(2)}) copy-start(bf16[512]{0:T(512)(128)(2,1)} %param.40) | copy-start | bytes 3076
  40.6 6.2 %copy-start.37 = (bf16[512]{0:T(512)(128)(2,1)S(1)}, bf16[512]{0:T(512)(128)(2,1)}, u32[]{:S(2)}) copy-start(bf16[512]{0:T(512)(128)(2,1)} %param.42) | copy-start | bytes 3076
  40.6 6.4 %copy-start.19 = (bf16[512,512]{1,0:T(8,128)(2,1)S(1)}, bf16[512,512]{1,0:T(8,128)(2,1)}, u32[]{:S(2)}) copy-start(bf16[512,512]{1,0:T(8,128)(2,1)} %param.43) | copy-start | bytes 1572868
  47.0 4.9 copy-start.8
  62.3 5.0 copy-start.9
  62.3 5.0 copy-start.17
  68.8 6.1 %copy-start.10 = (bf16[2,16,16,512]{3,2,1,0:T(8,128)(2,1)S(1)}, bf16[2,16,16,512]{3,2,1,0:T(8,128)(2,1)}, u32[]{:S(2)}) copy-start(bf16[2,16,16,512]{3,2,1,0:T(8,128)(2,1)} %copy-done.8) | copy-start | bytes 1572868
  74.9 4.6 copy-start.18
  122.7 3.7 copy-start.12
  139.6 4.3 copy-start.39
  139.6 5.9 %copy-start.16 = (bf16[2,16,16,512]{3,2,1,0:T(8,128)(2,1)S(1)}, bf16[2,16,16,512]{3,2,1,0:T(8,128)(2,1)}, u32[]{:S(2)}) copy-start(bf16[2,16,16,512]{3,2,1,0:T(8,128)(2,1)} %param.25) | copy-start | bytes 1572868
  145.5 10.0 %copy-start.30 = (s32[512]{0:T(512)S(1)}, s32[512]{0:T(512)}, u32[]{:S(2)}) copy-start(s32[512]{0:T(512)} %param.26) | copy-start | bytes 6148
  145.5 58.7 %copy-start.26 = (f32[32,256]{1,0:T(8,128)S(1)}, f32[32,256]{1,0:T(8,128)}, u32[]{:S(2)}) copy-start(f32[32,256]{1,0:T(8,128)} %param.30) | copy-start | bytes 98308
  149.5 5.2 all-to-all-start.1
  531.5 8.8 %copy-start.11 = (f32[3,3,512,512]{3,2,1,0:T(8,128)S(1)}, f32[3,3,512,512]{3,2,1,0:T(8,128)}, u32[]{:S(2)}) copy-start(f32[3,3,512,512]{3,2,1,0:T(8,128)} %get-tuple-element.82) | copy-start | bytes 28311556
  540.3 4.1 copy-start.24
  540.3 5.0 copy-start.23
  540.3 8.0 %copy-start.1 = (bf16[512,512]{1,0:T(8,128)(2,1)S(1)}, bf16[512,512]{1,0:T(8,128)(2,1)}, u32[]{:S(2)}) copy-start(bf16[512,512]{1,0:T(8,128)(2,1)} %param.44) | copy-start | bytes 1572868
  (17 other events, 38.5 us)
Sparse Core Ops, SparseCore 0:
  14.2 137.6 reduce-scatter.1
  160.6 370.8 all-reduce.7
where the time goes:
time: 564 us; the launch traced here: 556 us
  waiting for transfers between devices  326 us (58%)
  matrix products  69.9 us (12%)
  local copies, waits for them, and re-layouts  68.8 us (12%)
  blocking collectives  44.5 us (8%)
  other arithmetic  22.6 us (4%)
  between operations  17.2 us (3%)
  starting transfers between devices  7.2 us (1%)
    psum x1, waiting for transfers between devices, local(): lax.psum((first_gain_grad, first_offset_grad, conv1_kernel_grad, first_bi...  326 us
    psum x1, blocking collectives, local(): lax.psum((first_gain_grad, first_offset_grad, conv1_kernel_grad, first_bi...  44.5 us
    unnamed x98, local copies, waits for them, and re-layouts  41.5 us
    dot_general x36, matrix products, conv_taps(): lax.dot_general(window, kernel[tap_row, tap_col], (((3,), (0,)), ((), ())...  32.7 us
    reshape x2, local copies, waits for them, and re-layouts, group_norm(): grouped = source.reshape(images, height * across, G, channels // G)  11.4 us
  transfers between devices with their start and end apart: 4, of which 2 were waited for; matrix products, arithmetic and copies ran while one was open for 24% of the time, Pallas kernels for 0%

commit v1 on v0

--- a/solution.py
+++ b/solution.py
@@ -275,27 +275,30 @@
         out_weight_grad,
         out_bias_grad,
     ) = lax.psum(
-        (
-            first_gain_grad,
-            first_offset_grad,
-            conv1_kernel_grad,
-            first_bias_grad,
-            second_gain_grad,
-            second_offset_grad,
-            conv2_kernel_grad,
-            second_bias_grad,
-            counts,
-            third_gain_grad,
-            third_offset_grad,
-            query_weight_grad,
-            query_bias_grad,
-            key_weight_grad,
-            value_weight_grad,
-            value_bias_grad,
-            out_weight_grad,
-            out_bias_grad,
+        lax.psum(
+            (
+                first_gain_grad,
+                first_offset_grad,
+                conv1_kernel_grad,
+                first_bias_grad,
+                second_gain_grad,
+                second_offset_grad,
+                conv2_kernel_grad,
+                second_bias_grad,
+                counts,
+                third_gain_grad,
+                third_offset_grad,
+                query_weight_grad,
+                query_bias_grad,
+                key_weight_grad,
+                value_weight_grad,
+                value_bias_grad,
+                out_weight_grad,
+                out_bias_grad,
+            ),
+            "row",
         ),
-        ("grp", "row"),
+        "grp",
     )
     shares = counts / jnp.sum(counts)
     perplexity = jnp.exp(-jnp.sum(shares * jnp.log(shares + 1e-10)))

time: 564 us -> 860 us (1.52)
  waiting for transfers between devices: 326 us -> 590 us
  blocking collectives: 44.5 us -> 84.3 us
    psum x0 -> x1, waiting for transfers between devices: none -> 469 us  [local(): lax.psum(lax.psum((first_gain_grad, first_offset_grad, conv1_kernel_grad,...]
    psum x1, waiting for transfers between devices: 326 us -> 75.5 us  [local(): lax.psum((first_gain_grad, first_offset_grad, conv1_kernel_grad, first_bi...]
    psum x0 -> x1, blocking collectives: none -> 80.9 us  [local(): lax.psum(lax.psum((first_gain_grad, first_offset_grad, conv1_kernel_grad,...]
    reduce_scatter x1, waiting for transfers between devices: 0.01 us -> 44 us  [local(): lax.psum_scatter(jnp.dot(chosen, latents, preferred_element_type=jnp.floa...]
    psum x1, blocking collectives: 44.5 us -> 3.4 us  [local(): lax.psum((first_gain_grad, first_offset_grad, conv1_kernel_grad, first_bi...]
    unnamed x98 -> x120, local copies, waits for them, and re-layouts: 41.5 us -> 41.7 us
  transfers between devices with their start and end apart: 4 -> 5, of which waited for: 2 -> 5; matrix products, arithmetic and copies ran while one was open for 24% -> 4% of each run, Pallas kernels for 0% -> 0%
where the time goes in v1:
time: 860 us; the launch traced here: 853 us
  waiting for transfers between devices  590 us (69%)
  blocking collectives  84.3 us (10%)
  local copies, waits for them, and re-layouts  69 us (8%)
  matrix products  61.6 us (7%)
  other arithmetic  21.9 us (3%)
  between operations  18.8 us (2%)
    psum x1, waiting for transfers between devices, local(): lax.psum(lax.psum((first_gain_grad, first_offset_grad, conv1_kernel_grad,...  469 us
    psum x1, blocking collectives, local(): lax.psum(lax.psum((first_gain_grad, first_offset_grad, conv1_kernel_grad,...  80.9 us
    psum x1, waiting for transfers between devices, local(): lax.psum((first_gain_grad, first_offset_grad, conv1_kernel_grad, first_bi...  75.5 us
    reduce_scatter x1, waiting for transfers between devices, local(): lax.psum_scatter(jnp.dot(chosen, latents, preferred_element_type=jnp.floa...  44 us
    unnamed x120, local copies, waits for them, and re-layouts  41.7 us
    dot_general x36, matrix products, conv_taps(): lax.dot_general(window, kernel[tap_row, tap_col], (((3,), (0,)), ((), ())...  25.6 us
  transfers between devices with their start and end apart: 5, of which 5 were waited for; matrix products, arithmetic and copies ran while one was open for 4% of the time, Pallas kernels for 0%

profile of v1, /device:TPU:0, one launch (start us, length us, event | category | flops | bytes accessed | tf_op | source)
XLA Modules:
  0.0 852.6 jit_solution(7964240179336301901)
XLA Ops:
  8.1 3.6 all-to-all-start
  15.7 1.7 fusion.53
  32.3 5.3 reshape.298
  41.1 1.7 convolution_convert_fusion.1
  47.4 6.6 copy.106
  54.0 2.3 convolution_convert_fusion.2
  56.3 2.6 fusion.139
  60.4 6.1 copy.103
  66.4 2.5 fusion.141
  69.0 2.0 convolution_add_fusion.17
  74.0 2.5 copy.100
  76.6 2.9 reshape.297
  79.7 2.9 fusion.27
  83.0 2.8 reverse_bitcast_fusion.1
  91.3 1.9 fusion.133
  93.6 1.9 multiply_reduce_fusion.1
  95.8 1.9 convert_reduce_fusion.5
  105.3 3.3 copy-done.14
  111.9 3.7 copy-done.13
  119.6 75.5 %all-reduce.13.cloned.1.call-done = (f32[3,3,512,512]{3,2,1,0:T(8,128)}, f32[3,3,512,512]{3,2,1,0:T(8,128)}, f32[512,512]{1,0:T(8,128)}, f32[512,512]{1,0:T(8,12...) async-done(((f32[3,3,512,512]{3,2,1,0:T(8,128)}, f32[3,3,512,512]{3,2,1,0:T(8,128)}, f32[512,512]{1,0:T(8,128)}, f32[512,512]{1,0:T(8,128)}, f32[512,512]{1,0:T(8,128)}, ...) | async-done | bytes 23068688 | tf_op jit(solution)/shard_map/psum | solution.py:278
  195.1 6.8 copy.107
  201.9 2.7 reverse_bitcast_fusion
  208.4 1.9 fusion.134
  214.3 3.1 add_convert_fusion
  218.2 3.5 all-to-all-start.1
  224.5 3.4 all-reduce.6
  227.9 80.9 %all-reduce.4 = (f32[512]{0:T(512)}, f32[512]{0:T(512)}, f32[512]{0:T(512)}, f32[512]{0:T(512)}, f32[512]{0:T(512)}, /*index=5*/f32[512]{0:T(512)}, f32[512]{0:T...) all-reduce(f32[512]{0:T(512)S(1)} %get-tuple-element.50, ...), channel_id=1, replica_groups=mesh['grp'=16,'row'=2] {'grp'}, use_global_device_ids=true, to_apply=%region_28.29 | all-reduce | flops 6656 | bytes 53248 | tf_op jit(solution)/shard_map/psum | solution.py:277
  309.4 1.8 multiply_reduce_fusion.10
  312.7 44.0 %reduce-scatter.2.cloned.1.call-done = f32[32,256]{1,0:T(8,128)} async-done(((f32[1024,256]{1,0:T(8,128)}), f32[32,256]{1,0:T(8,128)}) %reduce-scatter.2.cloned.1.call-update) | async-done | bytes 32784 | tf_op jit(solution)/shard_map/reduce_scatter | solution.py:314
  358.2 468.9 %all-reduce.11.cloned.1.call-done = (f32[3,3,512,512]{3,2,1,0:T(8,128)}, f32[3,3,512,512]{3,2,1,0:T(8,128)}, f32[512,512]{1,0:T(8,128)}, f32[512,512]{1,0:T(8,12...) async-done(((f32[3,3,512,512]{3,2,1,0:T(8,128)}, f32[3,3,512,512]{3,2,1,0:T(8,128)}, f32[512,512]{1,0:T(8,128)}, f32[512,512]{1,0:T(8,128)}, f32[512,512]{1,0:T(8,128)}, ...) | async-done | bytes 23068688 | tf_op jit(solution)/shard_map/psum | solution.py:277
  827.1 8.8 %copy.197 = f32[3,3,512,512]{3,2,1,0:T(8,128)} copy(f32[3,3,512,512]{3,2,1,0:T(8,128)} %get-tuple-element.96) | data formatting | bytes 18874368
  835.9 4.1 copy.198
  (286 shorter events, 70.4 us)
Async XLA Ops:
  8.0 34.8 %copy-start = (bf16[512,512]{1,0:T(8,128)(2,1)S(1)}, bf16[512,512]{1,0:T(8,128)(2,1)}, u32[]{:S(2)}) copy-start(bf16[512,512]{1,0:T(8,128)(2,1)} %param.44) | copy-start | bytes 1572868
  8.0 6.1 copy-start.41
  8.1 7.2 copy-start.42
  8.1 7.2 copy-start.43
  8.1 5.4 all-to-all-start
  11.7 183.4 %all-reduce.13.cloned.1.call-start = ((), (), s32[]{:S(2)}) async-start(), calls=%async_computation.5 | async-start | bytes 46137344 | tf_op jit(solution)/shard_map/psum | solution.py:278
  12.4 7.3 copy-start.31
  13.6 5.3 copy-start.2
  14.2 5.6 copy-start.27
  14.2 5.6 copy-start.34
  15.3 4.5 copy-start.29
  22.5 6.0 copy-start.5
  23.4 6.6 slice-start
  25.4 4.6 slice-start.1
  32.3 6.2 copy-start.38
  32.3 6.2 copy-start.46
  32.3 6.2 copy-start.47
  32.3 6.4 copy-start.20
  38.7 4.9 copy-start.9
  54.0 4.9 copy-start.10
  54.0 4.9 copy-start.18
  60.4 6.1 copy-start.11
  66.4 4.6 copy-start.19
  117.1 239.6 %reduce-scatter.2.cloned.1.call-start = ((), (), s32[]{:S(2)}) async-start(), calls=%async_computation.3 | async-start | bytes 1081344 | tf_op jit(solution)/shard_map/reduce_scatter | solution.py:314
  119.6 707.5 %all-reduce.11.cloned.1.call-start = ((), (), s32[]{:S(2)}) async-start(), calls=%async_computation.4 | async-start | bytes 46137344 | tf_op jit(solution)/shard_map/psum | solution.py:277
  208.3 5.9 copy-start.17
  214.2 10.0 %copy-start.40 = (s32[512]{0:T(512)S(1)}, s32[512]{0:T(512)}, u32[]{:S(2)}) copy-start(s32[512]{0:T(512)} %param.26) | copy-start | bytes 6148
  214.3 142.5 %copy-start.33 = (f32[32,256]{1,0:T(8,128)S(1)}, f32[32,256]{1,0:T(8,128)}, u32[]{:S(2)}) copy-start(f32[32,256]{1,0:T(8,128)} %param.30) | copy-start | bytes 98308
  218.2 5.2 all-to-all-start.1
  827.1 8.8 %copy-start.12 = (f32[3,3,512,512]{3,2,1,0:T(8,128)S(1)}, f32[3,3,512,512]{3,2,1,0:T(8,128)}, u32[]{:S(2)}) copy-start(f32[3,3,512,512]{3,2,1,0:T(8,128)} %get-tuple-element.100) | copy-start | bytes 28311556
  835.9 5.0 copy-start.24
  835.9 8.0 copy-start.1
  (29 other events, 71.6 us)
Sparse Core Ops, SparseCore 0:
  117.2 77.7 all-reduce.12
  201.5 625.5 all-reduce.10
Sparse Core Ops, SparseCore 1:
  120.5 236.1 reduce-scatter.1
